TPU v7x, 32 devices: a whole 2x2x4 slice. The times are simulated.
32 devices in a mesh: ctx: 8 (over z, y), tp: 4 (over x, core).
Axes of the slice: x: 2, y: 2, z: 4, core: 2. Of those that a mesh axis runs over, the one named last changes fastest.
Arguments:
- features: bfloat16 [3, 1024, 4096], P(None, 'ctx', 'tp'), may hold values from -6 to 6
- out_grad: bfloat16 [1024, 4096], P('ctx', 'tp'), may hold values from -6 to 6
- attn_parts: bfloat16 [4, 1024, 4096], P('tp', 'ctx'), may hold values from -6 to 6
- short_filt: bfloat16 [3, 256, 7], P(None, 'tp'), may hold values from -2 to 2
- med_filt: bfloat16 [256, 128], P('tp'), may hold values from -0.5 to 0.5
- piece_home: int32 [32], replicated, may hold values from 0 to 7, as said below
- piece_start: int32 [32], replicated, may hold values from 0 to 96, as said below
Outputs:
- feat_grad: bfloat16 [3, 1024, 4096], P(None, 'ctx', 'tp')
- short_grad: float32 [3, 256, 7], P(None, 'tp')
- med_grad: float32 [256, 128], P('tp')
Inputs may be any that keep to these rules, and one draw needn't show every extreme that they name: `piece_home`: entry i * 4 + l names the home device of the piece of 32 rows that starts at row l * 32 of device i in the balanced layout. With piece_start the entries name every piece of every home device exactly once, and no device of the balanced layout holds two pieces of the same home device. `piece_start`: A multiple of 32.
All inputs are finite; a program needn't handle non-finite values.
Results may differ from a plain program's by a relative error of at most 0.012.
Values may be sent and summed in bfloat16 or wider, within the bound.
A program may use at most 64 MiB of HBM per device.

v0:
```python
import functools
import math

import jax
import jax.numpy as jnp
from jax import lax
from jax.experimental import pallas as pl
from jax.experimental.pallas import tpu as pltpu
from jax.sharding import PartitionSpec as P

GROUP = 16
MESH = pl.DeviceIdType.MESH
LANES = 256


def cost(flops, bytes_accessed):
    return pl.CostEstimate(flops=flops, bytes_accessed=bytes_accessed, transcendentals=0)


def plane(rows, axis):
    return lax.broadcasted_iota(jnp.int32, (rows, rows), axis)


def whole_kernel(
    n, tp, pick_ref, origin_ref, attn_ref, feat_ref, out_grad_ref, wt_ref, filt_ref, back_ref,
    feat_out, total_ref,
    streams_ref, kv_ref, before_ref, rim_ref, dmix_ref, ds_ref, after_ref,
    short_ref, flat_ref, part_ref, sums, gathered, head_ref, tail_in,
    got, passed, crossed, acc, pieces, stage, landed, rim_in, key_in, mix_in, ext,
    pair_send, pair_recv, cross_send, cross_recv, send, recv, halo_send, halo_recv,
    send1, recv1, send2, recv2,
):
    dq_ref = ds_ref.at[0]
    me = lax.axis_index("ctx")
    col = lax.axis_index("tp")
    f32 = jnp.float32
    rows, width = kv_ref.shape
    taps = wt_ref.shape[1]
    long_taps = filt_ref.shape[1]
    chunk = ext.shape[1]
    piece_rows = stage.shape[1]
    half = tp // 2
    blocks = got.shape[1]
    part = rows // blocks
    side, row = lax.rem(col, 2), col // 2
    partner = row * 2 + 1 - side
    barrier = pltpu.get_barrier_semaphore()

    def other(d):
        return lax.rem(row + d, half) * 2 + side

    def greet(k, carry):
        pl.semaphore_signal(
            barrier, inc=1, device_id={"ctx": lax.rem(me + k, n)}, device_id_type=MESH
        )
        return carry

    lax.fori_loop(1, n, greet, 0)
    pl.semaphore_signal(barrier, inc=1, device_id={"tp": partner}, device_id_type=MESH)
    for d in range(1, half):
        pl.semaphore_signal(barrier, inc=1, device_id={"tp": other(d)}, device_id_type=MESH)
    pl.semaphore_wait(barrier, n - 1 + half)

    def hop(source, target, at, by):
        return pltpu.make_async_remote_copy(
            source, target, halo_send.at[at], halo_recv.at[at],
            device_id={"ctx": lax.rem(me + by + n, n)}, device_id_type=MESH,
        )

    def slab(which, r):
        lane = pl.multiple_of(which * width, width)
        return attn_ref.at[pl.ds(r * part, part), pl.ds(lane, width)]

    def slab_value(which, r):
        lane = pl.multiple_of(which * width, width)
        return attn_ref[pl.ds(r * part, part), pl.ds(lane, width)].astype(f32)

    def pair(d, r):
        line = lax.rem(row + d, half)
        return pltpu.make_async_remote_copy(
            slab(line * 2 + 1 - side, r), got.at[d, r],
            pair_send.at[d, r], pair_recv.at[d, r],
            device_id={"tp": partner}, device_id_type=MESH,
        )

    def cross(d, r):
        return pltpu.make_async_remote_copy(
            passed.at[d, r], crossed.at[d, r], cross_send.at[d, r], cross_recv.at[d, r],
            device_id={"tp": other(d)}, device_id_type=MESH,
        )

    order = [d for d in range(1, half)] + [0]
    rim_hop = hop(feat_ref.at[:, pl.ds(rows - 16, 16), :], rim_in, 0, 1)
    rim_hop.start()
    for d in order:
        for r in range(blocks):
            pair(d, r).start()
    for d in range(1, half):
        for r in range(blocks):
            pair(d, r).wait()
            passed[d, r] = (slab_value(other(d), r) + got[d, r].astype(f32)).astype(got.dtype)
            cross(d, r).start()
    rim_hop.wait()
    first = me == 0
    last = me == n - 1
    rim_ref[...] = jnp.where(first, 0.0, rim_in[...].astype(f32)).astype(rim_ref.dtype)

    def stream_step(c, carry):
        cols = pl.ds(pl.multiple_of(c * chunk, chunk), chunk)
        found = []
        for s in range(3):
            ext[0:16] = rim_ref[s, :, cols].astype(f32)
            ext[16:] = feat_ref[s, :, cols].astype(f32)
            total = wt_ref[s, 0:1, cols] * ext[16:]
            for lag in range(1, taps):
                total = total + wt_ref[s, lag : lag + 1, cols] * ext[16 - lag : 16 - lag + rows]
            streams_ref[s, :, cols] = total
            found.append(total)
        kv_ref[:, cols] = (found[1] * found[2]).astype(kv_ref.dtype)
        return carry

    lax.fori_loop(0, width // chunk, stream_step, 0)
    key_hop = hop(kv_ref, key_in, 1, 1)
    key_hop.start()
    for r in range(blocks):
        pair(0, r).wait()
        total = slab_value(col, r) + got[0, r].astype(f32)
        for d in range(1, half):
            cross(d, r).wait()
            total = total + crossed[d, r].astype(f32)
        for i in range(part // piece_rows):
            pieces[r * (part // piece_rows) + i] = total[i * piece_rows : (i + 1) * piece_rows]

    def route(k):
        peer = lax.rem(me + k, n)
        return pltpu.make_async_remote_copy(
            stage.at[k], landed.at[k], send.at[k], recv.at[k],
            device_id={"ctx": peer}, device_id_type=MESH,
        )

    def piece(k):
        slot = pick_ref[lax.rem(me + k, n)]
        return pieces[slot].astype(stage.dtype)

    def send_step(k, carry):
        stage[k] = piece(k)
        route(k).start()
        return carry

    lax.fori_loop(1, n, send_step, 0)
    landed[0] = piece(0)
    key_hop.wait()
    before_ref[...] = jnp.where(first, 0.0, key_in[...].astype(f32)).astype(before_ref.dtype)
    t, s = plane(long_taps, 0), plane(long_taps, 1)
    owner = lax.broadcasted_iota(jnp.int32, (long_taps, chunk), 1) // GROUP

    def mixed_step(c, carry):
        cols = pl.ds(pl.multiple_of(c * chunk, chunk), chunk)
        window = jnp.concatenate([before_ref[:, cols], kv_ref[:, cols]], axis=0)
        total = jnp.zeros((long_taps, chunk), f32)
        for g in range(chunk // GROUP):
            line = jnp.broadcast_to(
                filt_ref[pl.ds(c * (chunk // GROUP) + g, 1), :], (long_taps, long_taps)
            )
            wheel = pltpu.roll(line, 0, 1, stride=1, stride_axis=0)
            table = jnp.concatenate(
                [jnp.where(s > t, wheel, 0.0), jnp.where(s <= t, wheel, 0.0)], axis=1
            ).astype(kv_ref.dtype)
            product = jnp.dot(table, window, preferred_element_type=f32)
            total = jnp.where(owner == g, product, total)
        dq_ref[:, cols] = total
        return carry

    lax.fori_loop(0, width // chunk, mixed_step, 0)

    def wait_step(k, carry):
        route(k).wait()
        return carry

    lax.fori_loop(1, n, wait_step, 0)

    for slot in range(rows // piece_rows):
        at = lax.rem(me - origin_ref[slot] + n, n)
        acc[slot * piece_rows : (slot + 1) * piece_rows] = landed[at].astype(f32)
    grad = out_grad_ref[...].astype(f32) + acc[...]
    dmix_ref[...] = (grad * streams_ref[0]).astype(dmix_ref.dtype)
    mix_hop = hop(dmix_ref, mix_in, 2, -1)
    mix_hop.start()
    dq_ref[...] = grad * dq_ref[...]
    kind = dmix_ref.dtype
    flip = jnp.where(t + s == long_taps - 1, 1.0, 0.0).astype(kind)
    near = chunk // GROUP

    def short_sums(k, cols, value):
        ext[0:16] = rim_ref[k, :, cols].astype(f32)
        ext[16:] = feat_ref[k, :, cols].astype(f32)
        for lag in range(taps):
            at = k * taps + lag
            short_ref[at : at + 1, cols] = jnp.sum(
                value * ext[16 - lag : 16 - lag + rows], axis=0, keepdims=True
            )

    def lag_step(c, carry):
        cols = pl.ds(pl.multiple_of(c * chunk, chunk), chunk)
        flipped = jnp.dot(flip, dmix_ref[:, cols], preferred_element_type=f32)
        window = jnp.concatenate([before_ref[:, cols], kv_ref[:, cols]], axis=0)
        for g in range(near):
            left = jnp.where(owner == g, flipped, 0.0).astype(kind)
            both = lax.dot_general(
                left, window, (((1,), (1,)), ((), ())), preferred_element_type=f32
            )
            ring = jnp.where(s + t <= long_taps - 1, both[:, long_taps:], both[:, :long_taps])
            ring = pltpu.roll(ring, 0, 1, stride=1, stride_axis=0)
            flat_ref[pl.ds(c * near + g, 1), :] = jnp.sum(ring, axis=0, keepdims=True)
        short_sums(0, cols, dq_ref[:, cols])
        return carry

    lax.fori_loop(0, width // chunk, lag_step, 0)
    mix_hop.wait()
    after_ref[...] = jnp.where(last, 0.0, mix_in[...].astype(f32)).astype(kind)

    def back_step(c, carry):
        cols = pl.ds(pl.multiple_of(c * chunk, chunk), chunk)
        window = jnp.concatenate([dmix_ref[:, cols], after_ref[:, cols]], axis=0)
        total = jnp.zeros((long_taps, chunk), f32)
        for g in range(near):
            line = jnp.broadcast_to(
                back_ref[pl.ds(c * near + g, 1), :], (long_taps, long_taps)
            )
            wheel = pltpu.roll(line, 0, 1, stride=1, stride_axis=0)
            table = jnp.concatenate(
                [jnp.where(s >= t, wheel, 0.0), jnp.where(s < t, wheel, 0.0)], axis=1
            ).astype(kind)
            product = jnp.dot(table, window, preferred_element_type=f32)
            total = jnp.where(owner == g, product, total)
        for k in (1, 2):
            value = total * streams_ref[3 - k, :, cols]
            ds_ref[k, :, cols] = value
            short_sums(k, cols, value)
        return carry

    lax.fori_loop(0, width // chunk, back_step, 0)
    head_ref[...] = ds_ref[:, 0:16, :].astype(kind)
    tail_hop = hop(head_ref, tail_in, 3, -1)
    tail_hop.start()
    groups = width // GROUP
    used = groups + 3 * taps
    member = jnp.where(
        lax.broadcasted_iota(jnp.int32, (width, long_taps), 0) // GROUP
        == lax.broadcasted_iota(jnp.int32, (width, long_taps), 1),
        1.0,
        0.0,
    )
    flat_ref[groups:used] = jnp.dot(
        short_ref[...], member, precision=lax.Precision.HIGHEST, preferred_element_type=f32
    )
    share = part_ref.shape[1]
    if n * share > used:
        flat_ref[used : n * share] = jnp.zeros((n * share - used, long_taps), f32)
    for k in range(n):
        part_ref[k] = flat_ref[k * share : (k + 1) * share]

    def scatter(k):
        peer = lax.rem(me + k, n)
        return pltpu.make_async_remote_copy(
            part_ref.at[peer], sums.at[k], send1.at[k], recv1.at[k],
            device_id={"ctx": peer}, device_id_type=MESH,
        )

    def gather(k):
        return pltpu.make_async_remote_copy(
            gathered.at[me], gathered.at[me], send2.at[k], recv2.at[k],
            device_id={"ctx": lax.rem(me + k, n)}, device_id_type=MESH,
        )

    def each(copy, act):
        def step(k, carry):
            act(copy(k))
            return carry

        lax.fori_loop(1, n, step, 0)

    def feat_step(k):
        def step(c, carry):
            cols = pl.ds(pl.multiple_of(c * chunk, chunk), chunk)
            ext[0:rows] = ds_ref[k, :, cols]
            ext[rows:] = jnp.where(last, 0.0, tail_in[k, :, cols].astype(f32))
            total = wt_ref[k, 0:1, cols] * ds_ref[k, :, cols]
            for lag in range(1, taps):
                total = total + wt_ref[k, lag : lag + 1, cols] * ext[lag : lag + rows]
            feat_out[k, :, cols] = total.astype(feat_out.dtype)
            return carry

        lax.fori_loop(0, width // chunk, step, 0)

    each(scatter, lambda c: c.start())
    sums[0] = part_ref[me]
    tail_hop.wait()
    feat_step(0)
    each(scatter, lambda c: c.wait())
    result = sums[0]
    for k in range(1, n):
        result = result + sums[k]
    gathered[me] = result
    each(gather, lambda c: c.start())
    feat_step(1)
    feat_step(2)
    each(gather, lambda c: c.wait())
    total_ref[...] = gathered[...]


def shards(features, out_grad, attn_parts, short_filt, med_filt, piece_home, piece_start):
    rows, width = out_grad.shape
    groups, taps = med_filt.shape
    short_taps = short_filt.shape[2]
    ctx_count = lax.axis_size("ctx")
    own_index = lax.axis_index("ctx")
    per_device = ctx_count // 2
    piece_rows = rows // per_device
    factor = 1.0 / math.sqrt(rows * ctx_count * GROUP)
    chunk = LANES if width % LANES == 0 else width
    f32, half = jnp.float32, features.dtype

    everyone = piece_home.reshape(ctx_count, per_device)
    positions = (piece_start // piece_rows).reshape(ctx_count, per_device)
    local_home = lax.dynamic_slice_in_dim(everyone, own_index, 1, 0)[0]
    device_ids = jnp.arange(ctx_count, dtype=jnp.int32)
    slot_ids = jnp.arange(per_device, dtype=jnp.int32)
    matches = local_home[None, :] == device_ids[:, None]
    send_slot = jnp.sum(jnp.where(matches, slot_ids[None, :], 0), axis=1)
    keyed = jnp.where(everyone == own_index, positions, -1)
    hits = jnp.any(keyed[:, :, None] == slot_ids[None, None, :], axis=1)
    source_of = jnp.sum(jnp.where(hits, device_ids[:, None], 0), axis=0)
    short_weights = jnp.transpose(jnp.repeat(short_filt, GROUP, axis=1), (0, 2, 1)).astype(f32)
    filt = med_filt.astype(f32)
    filt_back = jnp.roll(filt[:, ::-1], 1, axis=1)
    tp_count = lax.axis_size("tp")
    blocks = 2 if rows % 32 == 0 else 1
    vmem = pl.BlockSpec(memory_space=pltpu.VMEM)
    smem = pl.BlockSpec(memory_space=pltpu.SMEM)
    dma = pltpu.SemaphoreType.DMA
    lanes = jax.ShapeDtypeStruct((rows, width), half)
    crossing = pltpu.VMEM((tp_count // 2, blocks, rows // blocks, width), half)
    flags = dma((tp_count // 2, blocks))
    routed = pltpu.VMEM((ctx_count, piece_rows, width), half)
    used = groups + 3 * short_taps
    share = -(-used // ctx_count)
    parts = (ctx_count, share, taps)
    held = pltpu.VMEM((rows, width), half)
    heads = pltpu.VMEM((3, 16, width), half)
    wide = pltpu.VMEM((3, rows, width), f32)
    peers = dma((ctx_count,))
    feat_grad, totals = pl.pallas_call(
        functools.partial(whole_kernel, ctx_count, tp_count),
        in_specs=[smem, smem] + [vmem] * 6,
        out_specs=(vmem, vmem),
        out_shape=(
            jax.ShapeDtypeStruct((3, rows, width), half),
            jax.ShapeDtypeStruct(parts, f32),
        ),
        scratch_shapes=[
            wide, held, held, heads, held, wide, held,
            pltpu.VMEM((3 * short_taps, width), f32),
            pltpu.VMEM((ctx_count * share, taps), f32),
            pltpu.VMEM(parts, f32), pltpu.VMEM(parts, f32), pltpu.VMEM(parts, f32),
            heads, heads,
            crossing, crossing, crossing,
            pltpu.VMEM((rows, width), f32),
            pltpu.VMEM((per_device, piece_rows, width), f32),
            routed, routed,
            heads, held, held,
            pltpu.VMEM((rows + 16, chunk), f32),
            flags, flags, flags, flags,
            peers, peers, dma((4,)), dma((4,)),
            peers, peers, peers, peers,
        ],
        compiler_params=pltpu.CompilerParams(
            collective_id=0, has_side_effects=True, vmem_limit_bytes=48 * 1024 * 1024
        ),
        cost_estimate=cost(12 * groups * taps * taps * chunk, 40 * rows * width),
    )(
        send_slot.astype(jnp.int32), source_of.astype(jnp.int32), attn_parts[0], features,
        out_grad, short_weights, filt_back, filt,
    )
    flat_totals = totals.reshape(-1, taps)
    short_total = flat_totals[groups:used, :groups].reshape(3, short_taps, groups)
    return (
        feat_grad,
        jnp.transpose(short_total, (0, 2, 1)) * factor,
        flat_totals[:groups, ::-1] * factor,
    )


def solution(mesh):
    return jax.shard_map(
        shards,
        mesh=mesh,
        in_specs=(
            P(None, "ctx", "tp"),
            P("ctx", "tp"),
            P("tp", "ctx", None),
            P(None, "tp", None),
            P("tp", None),
            P(),
            P(),
        ),
        out_specs=(P(None, "ctx", "tp"), P(None, "tp", None), P("tp", None)),
        check_vma=False,
    )
```

profile of v0, /device:TPU:0, one launch (start us, length us, event | category | flops | bytes accessed | tf_op | source)
XLA Modules:
  0.0 61.3 jit_solution(1024370978288653382)
XLA Ops:
  0.6 0.0 copy-start
  0.6 0.8 %reshape.30 = s32[8,4]{1,0:T(8,128)S(1)} reshape(s32[32]{0:T(128)} %param.12) | data formatting | bytes 256 | tf_op jit(solution)/shard_map/reshape | solution.py:324
  1.5 0.7 %and_select_fusion = s32[32]{0:T(128)S(1)} fusion(s32[32]{0:T(128)} %param.13), kind=kLoop, calls=%fused_computation.9 | loop fusion | flops 480 | bytes 256 | tf_op jit(solution)/shard_map/jit(floor_divide)/jit(_where)/select_n | solution.py:325
  2.1 0.1 reshape.31
  2.2 0.0 copy-start.3
  2.2 0.1 copy.10
  2.3 0.1 select_reduce_fusion
  2.5 0.0 copy-start.1
  2.5 1.0 %broadcast_in_dim.35 = f32[3,64,16,7]{2,1,3,0:T(8,128)S(1)} broadcast(bf16[3,64,7]{1,2,0:T(8,128)(2,1)} %param.10), dimensions={0,1,3} | broadcast | bytes 88704 | tf_op jit(solution)/shard_map/broadcast_in_dim | solution.py:334
  3.5 0.4 convert_element_type.11
  3.9 0.0 copy-done.3
  3.9 0.1 slice.24
  3.9 0.1 slice.20
  4.0 0.1 pad_maximum_fusion.filt_ref
  4.1 0.0 copy-done
  4.1 0.0 copy-done.1
  4.1 0.0 copy-start.2
  4.1 0.9 %copy-done.2 = bf16[128,1024]{1,0:T(8,128)(2,1)S(1)} copy-done((bf16[128,1024]{1,0:T(8,128)(2,1)S(1)}, bf16[128,1024]{1,0:T(8,128)(2,1)}, u32[]{:S(2)}) %copy-start.2) | copy-done | bytes 262168
  5.1 53.9 %shard_map.94 = (bf16[3,128,1024]{2,1,0:T(8,128)(2,1)S(1)}, f32[8,11,128]{2,1,0:T(8,128)S(1)}) custom-call(s32[8]{0:T(128)S(1)} %get-tuple-element.8.pick_ref, s32[4]{0:T(128)S(1)} %get-tuple-element.7.origin_ref, bf16[128,4096]{1,0:T(8,128)(2,1)S(1)} %bitcast.10, bf16[3,128,1024]{2,1,0:T(8,128)(2,1)S(1)} %copy-done.1, bf16[128,1024]{1,0:T(8,128)(2,1)S(1)} %copy-done.2, ...), custom_call_target="tpu_custom_call" | custom-call | flops 3221225472 | bytes 5242880 | tf_op jit(solution)/shard_map/pallas_call | solution.py:353
  59.1 0.1 rev.4
  59.1 0.6 %broadcast_multiply_fusion = f32[64,128]{1,0:T(8,128)} fusion(f32[64,128]{1,0:T(8,128)S(1)} %rev.4), kind=kLoop, calls=%fused_computation.1 | loop fusion | flops 8192 | bytes 65536 | tf_op jit(solution)/shard_map/mul | solution.py:390
  59.8 0.6 mul.20
  60.4 0.9 %copy.12 = bf16[3,128,1024]{2,1,0:T(8,128)(2,1)} copy(bf16[3,128,1024]{2,1,0:T(8,128)(2,1)S(1)} %get-tuple-element.12) | data formatting | bytes 1572864
  (8 shorter events, 0.1 us)
Async XLA Ops:
  0.6 3.5 %copy-start = (bf16[1,128,4096]{2,1,0:T(8,128)(2,1)S(1)}, bf16[1,128,4096]{2,1,0:T(8,128)(2,1)}, u32[]{:S(2)}) copy-start(bf16[1,128,4096]{2,1,0:T(8,128)(2,1)} %param.9) | copy-start | bytes 3145732
  2.2 1.6 %copy-start.3 = (bf16[64,128]{1,0:T(8,128)(2,1)S(1)}, bf16[64,128]{1,0:T(8,128)(2,1)}, u32[]{:S(2)}) copy-start(bf16[64,128]{1,0:T(8,128)(2,1)} %param.11) | copy-start | bytes 49156
  2.5 1.7 %copy-start.1 = (bf16[3,128,1024]{2,1,0:T(8,128)(2,1)S(1)}, bf16[3,128,1024]{2,1,0:T(8,128)(2,1)}, u32[]{:S(2)}) copy-start(bf16[3,128,1024]{2,1,0:T(8,128)(2,1)} %feat_ref.1) | copy-start | bytes 2359300
  4.1 1.0 %copy-start.2 = (bf16[128,1024]{1,0:T(8,128)(2,1)S(1)}, bf16[128,1024]{1,0:T(8,128)(2,1)}, u32[]{:S(2)}) copy-start(bf16[128,1024]{1,0:T(8,128)(2,1)} %out_grad_ref.1) | copy-start | bytes 786436
where the time goes:
time: 61.5 us; the launch traced here: 61.3 us
  Pallas kernels  53.9 us (88%)
  local copies, waits for them, and re-layouts  5.04 us (8%)
  other arithmetic  1.54 us (3%)
  between operations  0.73 us (1%)
    pallas_call x1, Pallas kernels, shards(): pl.pallas_call(functools.partial(whole_kernel, ctx_count, tp_count), in_s...  53.9 us
    unnamed x9, local copies, waits for them, and re-layouts  1.84 us

commit v1 on v0

v1 whole, which is shorter than its diff:
```python
import functools
import math

import jax
import jax.numpy as jnp
from jax import lax
from jax.experimental import pallas as pl
from jax.experimental.pallas import tpu as pltpu
from jax.sharding import PartitionSpec as P

GROUP = 16
MESH = pl.DeviceIdType.MESH
LANES = 256
EDGE = 8


def cost(flops, bytes_accessed):
    return pl.CostEstimate(flops=flops, bytes_accessed=bytes_accessed, transcendentals=0)


def plane(rows, axis):
    return lax.broadcasted_iota(jnp.int32, (rows, rows), axis)


def whole_kernel(
    n, tp, inline, factor,
    home_hbm, start_hbm, attn_hbm, feat_hbm, grad_hbm, taps_hbm, med_hbm,
    feat_out, short_out, med_out,
    home, start, feat_ref, out_grad_ref, mine_ref, taps_ref, med_ref,
    wt_ref, filt_ref, back_ref, member_ref, ext, short_ref,
    streams_ref, kv_ref, before_ref, dmix_ref, ds_ref, acc,
    got, passed, crossed, pieces, stage, landed, ready,
    rim_in, key_in, mix_in, head_ref, tail_in,
    flat_ref, part_ref, sums, gathered, last_ref, last_in, late_ref, late_in,
    local, pair_send, pair_recv, cross_send, cross_recv, send, recv, rim_sems, halo_send, halo_recv,
    send1, recv1, send2, recv2, send3, recv3, send4, recv4,
):
    me = lax.axis_index("ctx")
    col = lax.axis_index("tp")
    f32 = jnp.float32
    nc, rows, chunk = kv_ref.shape
    width = nc * chunk
    taps = taps_ref.shape[1]
    groups, long_taps = med_ref.shape
    per_device, piece_rows = pieces.shape[1:3]
    near = chunk // GROUP
    half = tp // 2
    side, row = lax.rem(col, 2), col // 2
    partner = row * 2 + 1 - side
    kind = kv_ref.dtype
    first = me == 0
    last = me == n - 1
    barrier = pltpu.get_barrier_semaphore()

    def other(d):
        return lax.rem(row + d, half) * 2 + side

    def peers(act):
        def step(k, carry):
            act(k)
            return carry

        lax.fori_loop(1, n, step, 0)

    def greet(k):
        pl.semaphore_signal(
            barrier, inc=1, device_id={"ctx": lax.rem(me + k, n)}, device_id_type=MESH
        )

    peers(greet)
    pl.semaphore_signal(barrier, inc=1, device_id={"tp": partner}, device_id_type=MESH)
    for d in range(1, half):
        pl.semaphore_signal(barrier, inc=1, device_id={"tp": other(d)}, device_id_type=MESH)

    def slab(which):
        return pl.ds(pl.multiple_of(which * width, width), width)

    def part(which, q):
        return pl.ds(pl.multiple_of(which * width + q * chunk, chunk), chunk)

    loads = [
        pltpu.make_async_copy(source, target, local.at[i])
        for i, (source, target) in enumerate(
            [
                (taps_hbm, taps_ref), (med_hbm, med_ref), (feat_hbm, feat_ref),
                (home_hbm, home), (start_hbm, start), (grad_hbm, out_grad_ref),
            ]
            + [
                (attn_hbm.at[:, slab(other(d))], mine_ref.at[d]) for d in range(half)
            ]
        )
    ]
    for load in loads:
        load.start()

    def hop(source, target, by, sends, recvs):
        return pltpu.make_async_remote_copy(
            source, target, sends, recvs,
            device_id={"ctx": lax.rem(me + by + n, n)}, device_id_type=MESH,
        )

    def key_hop(q):
        return hop(kv_ref.at[q], key_in.at[q], 1, halo_send.at[0, q], halo_recv.at[0, q])

    def mix_hop(q):
        return hop(dmix_ref.at[q], mix_in.at[q], -1, halo_send.at[1, q], halo_recv.at[1, q])

    def tail_hop(q):
        return hop(head_ref.at[q], tail_in.at[q], -1, halo_send.at[2, q], halo_recv.at[2, q])

    def pair(d, q):
        line = lax.rem(row + d, half)
        return pltpu.make_async_remote_copy(
            attn_hbm.at[:, part(line * 2 + 1 - side, q)], got.at[d, q],
            pair_send.at[d, q], pair_recv.at[d, q],
            device_id={"tp": partner}, device_id_type=MESH,
        )

    def cross(d, q):
        return pltpu.make_async_remote_copy(
            passed.at[d, q], crossed.at[d, q], cross_send.at[d, q], cross_recv.at[d, q],
            device_id={"tp": other(d)}, device_id_type=MESH,
        )

    def route(q, k):
        return pltpu.make_async_remote_copy(
            stage.at[q, k], landed.at[q, k], send.at[q, k], recv.at[q, k],
            device_id={"ctx": lax.rem(me + k, n)}, device_id_type=MESH,
        )

    def scatter(k):
        peer = lax.rem(me + k, n)
        return pltpu.make_async_remote_copy(
            part_ref.at[peer], sums.at[k], send1.at[k], recv1.at[k],
            device_id={"ctx": peer}, device_id_type=MESH,
        )

    def gather(k):
        return pltpu.make_async_remote_copy(
            gathered.at[me], gathered.at[me], send2.at[k], recv2.at[k],
            device_id={"ctx": lax.rem(me + k, n)}, device_id_type=MESH,
        )

    def share_last(k):
        return pltpu.make_async_remote_copy(
            last_ref, last_in.at[k], send3.at[k], recv3.at[k],
            device_id={"ctx": lax.rem(me + k, n)}, device_id_type=MESH,
        )

    def share_late(k):
        return pltpu.make_async_remote_copy(
            late_ref, late_in.at[k], send4.at[k], recv4.at[k],
            device_id={"ctx": lax.rem(me + k, n)}, device_id_type=MESH,
        )

    def columns(q):
        return pl.ds(pl.multiple_of(q * chunk, chunk), chunk)

    def chunks(low, high, act):
        def step(q, carry):
            act(q)
            return carry

        lax.fori_loop(low, high, step, 0)

    loads[0].wait()
    loads[1].wait()
    spread = jnp.where(
        lax.broadcasted_iota(jnp.int32, (groups, width), 0)
        == lax.broadcasted_iota(jnp.int32, (groups, width), 1) // GROUP,
        1.0,
        0.0,
    ).astype(kind)
    for s in range(3):
        wt_ref[s, 0:taps] = jnp.dot(taps_ref[s], spread, preferred_element_type=f32)
    t, s = plane(long_taps, 0), plane(long_taps, 1)
    turn = jnp.where((t + s == 0) | (t + s == long_taps), 1.0, 0.0).astype(kind)
    filt_ref[...] = jnp.dot(med_ref[...], turn, preferred_element_type=f32)
    back_ref[...] = med_ref[...].astype(f32)
    owned = lax.broadcasted_iota(jnp.int32, (width, long_taps), 0) // GROUP
    lane = lax.broadcasted_iota(jnp.int32, (width, long_taps), 1)
    member_ref[0] = jnp.where(owned == lane, 1.0, 0.0).astype(kind)
    member_ref[1] = jnp.where(owned + groups == lane, 1.0, 0.0).astype(kind)
    short_ref[...] = jnp.zeros_like(short_ref)
    last_ref[...] = jnp.zeros_like(last_ref)
    late_ref[...] = jnp.zeros_like(late_ref)
    loads[2].wait()

    def stream(k, cols, count):
        total = wt_ref[k, 0:1, cols] * ext[EDGE : EDGE + count]
        for lag in range(1, taps):
            total = total + wt_ref[k, lag : lag + 1, cols] * ext[EDGE - lag : EDGE - lag + count]
        return total

    def stream_step(q):
        cols = columns(q)
        found = []
        for k in range(3):
            ext[0:EDGE] = jnp.zeros((EDGE, chunk), f32)
            ext[EDGE : EDGE + rows] = feat_ref[k, :, cols].astype(f32)
            found.append(stream(k, cols, rows))
            streams_ref[k, :, cols] = found[k]
        kv_ref[q] = (found[1] * found[2]).astype(kind)

    chunks(0, nc, stream_step)
    pl.semaphore_wait(barrier, n - 1 + half)

    rim_hop = hop(
        feat_hbm.at[:, pl.ds(rows - EDGE, EDGE), :], rim_in, 1, rim_sems.at[0], rim_sems.at[1]
    )
    rim_hop.start()
    for d in [d for d in range(1, half)] + [0]:
        chunks(0, nc, lambda q, d=d: pair(d, q).start())

    for d in range(1, half):
        loads[6 + d].wait()

        def pass_on(q, d=d):
            pair(d, q).wait()
            passed[d, q] = (
                mine_ref[d, :, columns(q)].astype(f32) + got[d, q].astype(f32)
            ).astype(kind)
            cross(d, q).start()

        chunks(0, nc, pass_on)

    loads[3].wait()
    loads[4].wait()
    loads[6].wait()
    if inline:

        def pick(peer):
            slot = jnp.int32(0)
            for i in range(per_device):
                slot = jnp.where(home[me * per_device + i] == peer, i, slot)
            return slot

        def origin_of(slot):
            source = jnp.int32(0)
            for i in range(n * per_device):
                hit = (home[i] == me) & (start[i] == slot * piece_rows)
                source = jnp.where(hit, i // per_device, source)
            return source

        origins = [origin_of(slot) for slot in range(per_device)]
    else:

        def pick(peer):
            return home[peer]

        origins = [start[slot] for slot in range(per_device)]

    rim_hop.wait()

    def fill(k, cols, count):
        ext[0:EDGE] = jnp.where(first, 0.0, rim_in[k, :, cols].astype(f32))
        ext[EDGE : EDGE + count] = feat_ref[k, 0:count, cols].astype(f32)

    def send_step(q):
        cols = columns(q)
        found = []
        for k in range(3):
            fill(k, cols, GROUP)
            found.append(stream(k, cols, GROUP))
            streams_ref[k, 0:GROUP, cols] = found[k]
        kv_ref[q, 0:GROUP] = (found[1] * found[2]).astype(kind)
        key_hop(q).start()
        pair(0, q).wait()
        total = mine_ref[0, :, cols].astype(f32) + got[0, q].astype(f32)
        for d in range(1, half):
            cross(d, q).wait()
            total = total + crossed[d, q].astype(f32)
        for i in range(per_device):
            pieces[q, i] = total[i * piece_rows : (i + 1) * piece_rows]

        def launch(k):
            stage[q, k] = pieces[q, pick(lax.rem(me + k, n))].astype(kind)
            route(q, k).start()

        peers(launch)
        landed[q, 0] = pieces[q, pick(me)].astype(kind)

    chunks(0, nc, send_step)
    loads[5].wait()
    owner = lax.broadcasted_iota(jnp.int32, (long_taps, chunk), 1) // GROUP
    flip = jnp.where(t + s == long_taps - 1, 1.0, 0.0).astype(kind)

    def banded(lines, q, window, near_mask):
        total = jnp.zeros((long_taps, chunk), f32)
        for g in range(near):
            line = jnp.broadcast_to(lines[pl.ds(q * near + g, 1), :], (long_taps, long_taps))
            wheel = pltpu.roll(line, 0, 1, stride=1, stride_axis=0)
            table = jnp.concatenate(
                [jnp.where(near_mask, wheel, 0.0), jnp.where(near_mask, 0.0, wheel)], axis=1
            ).astype(kind)
            product = jnp.dot(table, window, preferred_element_type=f32)
            total = jnp.where(owner == g, product, total)
        return total

    def short_sums(k, q, value):
        cols = columns(q)
        fill(k, cols, rows)
        for lag in range(taps):
            short_ref[lag : lag + 1] = jnp.sum(
                value * ext[EDGE - lag : EDGE - lag + rows], axis=0, keepdims=True
            )
        exact = short_ref[...]
        high = exact.astype(kind)
        rest = exact - high.astype(f32)
        middle = rest.astype(kind)
        low = (rest - middle.astype(f32)).astype(kind)
        found = jnp.zeros((EDGE, long_taps), f32)
        for term in (high, middle, low):
            found = found + jnp.dot(
                term, member_ref[1 if k == 2 else 0, cols, :], preferred_element_type=f32
            )
        return found

    def receive(q, lines):
        cols = columns(q)
        peers(lambda k: route(q, k).wait())
        ready[...] = landed[q]
        for slot in range(per_device):
            at = lax.rem(me - origins[slot] + n, n)
            acc[slot * piece_rows : (slot + 1) * piece_rows] = ready[at].astype(f32)
        acc[...] = out_grad_ref[:, cols].astype(f32) + acc[...]
        dmix_ref[q] = (acc[...] * streams_ref[0, :, cols]).astype(kind)
        mix_hop(q).start()
        key_hop(q).wait()
        before_ref[...] = jnp.where(first, 0.0, key_in[q].astype(f32)).astype(kind)
        window = jnp.concatenate([before_ref[...], kv_ref[q]], axis=0)
        flipped = jnp.dot(flip, dmix_ref[q], preferred_element_type=f32)
        for g in range(near):
            left = jnp.where(owner == g, flipped, 0.0).astype(kind)
            both = lax.dot_general(
                left, window, (((1,), (1,)), ((), ())), preferred_element_type=f32
            )
            ring = jnp.where(s + t <= long_taps - 1, both[:, long_taps:], both[:, :long_taps])
            ring = pltpu.roll(ring, 0, 1, stride=1, stride_axis=0)
            lines(g, jnp.sum(ring, axis=0, keepdims=True))
        value = acc[...] * banded(filt_ref, q, window, s > t)
        ds_ref[0, :, cols] = value
        last_ref[near : near + EDGE] = last_ref[near : near + EDGE] + short_sums(0, q, value)

    def early(q):
        def lines(g, line):
            flat_ref[pl.ds(q * near + g, 1), :] = line

        receive(q, lines)

    def final_lines(g, line):
        last_ref[g : g + 1] = line

    def back_step(q):
        cols = columns(q)
        mix_hop(q).wait()
        after = jnp.where(last, 0.0, mix_in[q].astype(f32)).astype(kind)
        window = jnp.concatenate([dmix_ref[q], after], axis=0)
        total = banded(back_ref, q, window, s >= t)
        for k in (1, 2):
            value = total * streams_ref[3 - k, :, cols]
            ds_ref[k, :, cols] = value
            late_ref[...] = late_ref[...] + short_sums(k, q, value)
        head_ref[q] = ds_ref[:, 0:EDGE, cols].astype(kind)
        tail_hop(q).start()

    def feat_step(q):
        cols = columns(q)
        tail_hop(q).wait()
        for k in range(3):
            ext[0:rows] = ds_ref[k, :, cols]
            ext[rows:] = jnp.where(last, 0.0, tail_in[q, k].astype(f32))
            total = wt_ref[k, 0:1, cols] * ds_ref[k, :, cols]
            for lag in range(1, taps):
                total = total + wt_ref[k, lag : lag + 1, cols] * ext[lag : lag + rows]
            feat_out[k, :, cols] = total.astype(feat_out.dtype)

    share = part_ref.shape[1]
    used = (nc - 1) * near

    early(0)

    def both_steps(q):
        early(q)
        back_step(q - 1)

    chunks(1, nc - 1, both_steps)
    if n * share > used:
        flat_ref[used : n * share] = jnp.zeros((n * share - used, long_taps), f32)
    for k in range(n):
        part_ref[k] = flat_ref[k * share : (k + 1) * share]
    peers(lambda k: scatter(k).start())
    sums[0] = part_ref[me]
    receive(nc - 1, final_lines)
    peers(lambda k: share_last(k).start())
    peers(lambda k: scatter(k).wait())
    result = sums[0]
    for k in range(1, n):
        result = result + sums[k]
    gathered[me] = result
    peers(lambda k: gather(k).start())
    chunks(nc - 2, nc, back_step)
    peers(lambda k: share_late(k).start())
    chunks(0, nc, feat_step)
    peers(lambda k: gather(k).wait())
    for k in range(n):
        flat_ref[k * share : (k + 1) * share] = gathered[k]
    peers(lambda k: share_last(k).wait())
    total = last_ref[...]
    for k in range(1, n):
        total = total + last_in[k]
    flat_ref[used:groups] = total[0:near]
    mirror = jnp.where(t + s == long_taps - 1, 1.0, 0.0)
    med_out[...] = factor * jnp.dot(
        flat_ref[0:groups], mirror, precision=lax.Precision.HIGHEST, preferred_element_type=f32
    )
    peers(lambda k: share_late(k).wait())
    late = late_ref[...]
    for k in range(1, n):
        late = late + late_in[k]
    short_out[0] = factor * total[near : near + taps, :groups]
    short_out[1] = factor * late[:taps, :groups]
    short_out[2] = factor * late[:taps, groups : 2 * groups]


def store_kernel(feat_ref, short_ref, med_ref, feat_out, short_out, med_out, sems):
    copies = [
        pltpu.make_async_copy(source, target, sems.at[i])
        for i, (source, target) in enumerate(
            [(feat_ref, feat_out), (short_ref, short_out), (med_ref, med_out)]
        )
    ]
    for copy in copies:
        copy.start()
    for copy in copies:
        copy.wait()


def tables(piece_home, piece_start, ctx_count, per_device, piece_rows):
    own_index = lax.axis_index("ctx")
    everyone = piece_home.reshape(ctx_count, per_device)
    positions = (piece_start // piece_rows).reshape(ctx_count, per_device)
    local_home = lax.dynamic_slice_in_dim(everyone, own_index, 1, 0)[0]
    device_ids = jnp.arange(ctx_count, dtype=jnp.int32)
    slot_ids = jnp.arange(per_device, dtype=jnp.int32)
    matches = local_home[None, :] == device_ids[:, None]
    send_slot = jnp.sum(jnp.where(matches, slot_ids[None, :], 0), axis=1)
    keyed = jnp.where(everyone == own_index, positions, -1)
    hits = jnp.any(keyed[:, :, None] == slot_ids[None, None, :], axis=1)
    source_of = jnp.sum(jnp.where(hits, device_ids[:, None], 0), axis=0)
    return send_slot.astype(jnp.int32), source_of.astype(jnp.int32)


def shards(features, out_grad, attn_parts, short_filt, med_filt, piece_home, piece_start):
    rows, width = out_grad.shape
    groups, taps = med_filt.shape
    short_taps = short_filt.shape[2]
    ctx_count = lax.axis_size("ctx")
    tp_count = lax.axis_size("tp")
    per_device = ctx_count // 2
    piece_rows = rows // per_device
    factor = 1.0 / math.sqrt(rows * ctx_count * GROUP)
    chunk = LANES
    nc = width // chunk
    near = chunk // GROUP
    f32, half = jnp.float32, features.dtype
    inline = ctx_count * per_device <= 64
    if inline:
        home, start = piece_home, piece_start
    else:
        home, start = tables(piece_home, piece_start, ctx_count, per_device, piece_rows)

    vmem = pl.BlockSpec(memory_space=pltpu.VMEM)
    hbm = pl.BlockSpec(memory_space=pltpu.HBM)
    dma = pltpu.SemaphoreType.DMA
    share = -(-((nc - 1) * near) // ctx_count)
    parts = pltpu.VMEM((ctx_count, share, taps), f32)
    held = pltpu.VMEM((nc, rows, chunk), half)
    wide = pltpu.VMEM((3, rows, width), f32)
    crossing = pltpu.VMEM((tp_count // 2, nc, rows, chunk), half)
    routed = pltpu.VMEM((nc, ctx_count, piece_rows, chunk), half)
    heads = pltpu.VMEM((nc, 3, EDGE, chunk), half)
    flags = dma((tp_count // 2, nc))
    lanes = dma((nc, ctx_count))
    peers = dma((ctx_count,))
    outs = (
        jax.ShapeDtypeStruct((3, rows, width), half),
        jax.ShapeDtypeStruct((3, short_taps, groups), f32),
        jax.ShapeDtypeStruct((groups, taps), f32),
    )
    found = pl.pallas_call(
        functools.partial(whole_kernel, ctx_count, tp_count, inline, factor),
        in_specs=[hbm] * 7,
        out_specs=(vmem,) * 3,
        out_shape=outs,
        scratch_shapes=[
            pltpu.SMEM(home.shape, jnp.int32), pltpu.SMEM(start.shape, jnp.int32),
            pltpu.VMEM((3, rows, width), half), pltpu.VMEM((rows, width), half),
            pltpu.VMEM((tp_count // 2, rows, width), half),
            pltpu.VMEM((3, short_taps, groups), half), pltpu.VMEM((groups, taps), half),
            pltpu.VMEM((3, 8, width), f32), pltpu.VMEM((groups, taps), f32),
            pltpu.VMEM((groups, taps), f32), pltpu.VMEM((2, width, taps), half),
            pltpu.VMEM((rows + EDGE, chunk), f32), pltpu.VMEM((EDGE, chunk), f32),
            wide, held, pltpu.VMEM((rows, chunk), half), held, wide,
            pltpu.VMEM((rows, chunk), f32),
            crossing, crossing, crossing,
            pltpu.VMEM((nc, per_device, piece_rows, chunk), f32), routed, routed,
            pltpu.VMEM((ctx_count, piece_rows, chunk), half),
            pltpu.VMEM((3, EDGE, width), half), held, held, heads, heads,
            pltpu.VMEM((max(groups, ctx_count * share), taps), f32), parts, parts, parts,
            pltpu.VMEM((near + EDGE, taps), f32), pltpu.VMEM((ctx_count, near + EDGE, taps), f32),
            pltpu.VMEM((EDGE, taps), f32), pltpu.VMEM((ctx_count, EDGE, taps), f32),
            dma((6 + tp_count // 2,)), flags, flags, flags, flags, lanes, lanes,
            dma((2,)), dma((3, nc)), dma((3, nc)),
            peers, peers, peers, peers, peers, peers, peers, peers,
        ],
        compiler_params=pltpu.CompilerParams(
            collective_id=0, has_side_effects=True, vmem_limit_bytes=36 * 1024 * 1024
        ),
        cost_estimate=cost(12 * groups * taps * taps * chunk, 40 * rows * width),
    )(
        *[
            pltpu.with_memory_space_constraint(x, pltpu.HBM)
            for x in (
                home, start, attn_parts[0], features, out_grad,
                jnp.transpose(short_filt, (0, 2, 1)), med_filt,
            )
        ]
    )
    feat_grad, short_grad, med_grad = pl.pallas_call(
        store_kernel,
        in_specs=[vmem] * 3,
        out_specs=(hbm,) * 3,
        out_shape=outs,
        scratch_shapes=[dma((3,))],
        compiler_params=pltpu.CompilerParams(vmem_limit_bytes=4 * 1024 * 1024),
        cost_estimate=cost(0, 8 * rows * width),
    )(*found)
    return feat_grad, jnp.transpose(short_grad, (0, 2, 1)), med_grad


def solution(mesh):
    return jax.shard_map(
        shards,
        mesh=mesh,
        in_specs=(
            P(None, "ctx", "tp"),
            P("ctx", "tp"),
            P("tp", "ctx", None),
            P(None, "tp", None),
            P("tp", None),
            P(),
            P(),
        ),
        out_specs=(P(None, "ctx", "tp"), P(None, "tp", None), P("tp", None)),
        check_vma=False,
    )
```

time: 61.5 us -> 45 us (0.73)
  Pallas kernels: 53.9 us -> 44.2 us
  local copies, waits for them, and re-layouts: 5.04 us -> 0 us
  other arithmetic: 1.54 us -> 0 us
    pallas_call x1 -> x2, Pallas kernels: 53.9 us -> 44.2 us  [the longest x1 43.3 us: shards(): pl.pallas_call(functools.partial(whole_kernel, ctx_count, tp_count, inlin...]
    unnamed x9 -> x0, local copies, waits for them, and re-layouts: 1.84 us -> none
    broadcast_in_dim x1 -> x0, local copies, waits for them, and re-layouts: 1 us -> none  [shards(): jnp.repeat(short_filt, GROUP, axis=1)]
    reshape x3 -> x0, local copies, waits for them, and re-layouts: 0.9 us -> none  [the longest x1 0.82 us: shards(): everyone = piece_home.reshape(ctx_count, per_device)]
    select_n x2 -> x0, other arithmetic: 0.67 us -> none  [the longest x1 0.67 us: shards(): positions = (piece_start // piece_rows).reshape(ctx_count, per_device)]
    mul x2 -> x0, other arithmetic: 0.63 us -> none  [the longest x1 0.63 us: shards(): flat_totals[:groups, ::-1] * factor]
where the time goes in v1:
time: 45 us; the launch traced here: 44.8 us
  Pallas kernels  44.2 us (98%)
  between operations  0.64 us (1%)
    pallas_call x1, Pallas kernels, shards(): pl.pallas_call(functools.partial(whole_kernel, ctx_count, tp_count, inlin...  43.3 us
    pallas_call x1, Pallas kernels, shards(): pl.pallas_call(store_kernel, in_specs=[vmem] * 3, out_specs=(hbm,) * 3, o...  0.91 us

profile of v1, /device:TPU:0, one launch (start us, length us, event | category | flops | bytes accessed | tf_op | source)
XLA Modules:
  0.0 44.8 jit_solution(6584865387570117156)
XLA Ops:
  0.6 43.3 %shard_map.94 = (bf16[3,128,1024]{2,1,0:T(8,128)(2,1)S(1)}, f32[3,7,64]{2,1,0:T(8,128)S(1)}, f32[64,128]{1,0:T(8,128)S(1)}) custom-call(s32[32]{0:T(128)} %home_hbm.1, s32[32]{0:T(128)} %start_hbm.1, bf16[128,4096]{1,0:T(8,128)(2,1)} %bitcast.3, bf16[3,128,1024]{2,1,0:T(8,128)(2,1)} %feat_hbm.1, bf16[128,1024]{1,0:T(8,128)(2,1)} %grad_hbm.1, ...), custom_call_target="tpu_custom_call" | custom-call | flops 3221225472 | bytes 5242880 | tf_op jit(solution)/shard_map/pallas_call | solution.py:491
  43.9 0.9 %shard_map.95 = (bf16[3,128,1024]{2,1,0:T(8,128)(2,1)}, f32[3,7,64]{2,1,0:T(8,128)}, f32[64,128]{1,0:T(8,128)}) custom-call(bf16[3,128,1024]{2,1,0:T(8,128)(2,1)S(1)} %get-tuple-element.9.feat_ref, f32[3,7,64]{2,1,0:T(8,128)S(1)} %get-tuple-element.10.short_ref, f32[64,128]{1,0:T(8,128)S(1)} %get-tuple-element.11.med_ref), custom_call_target="tpu_custom_call" | custom-call | bytes 1048576 | tf_op jit(solution)/shard_map/pallas_call | solution.py:530

commit v2 on v1

--- a/solution.py
+++ b/solution.py
@@ -28,7 +28,7 @@
     feat_out, short_out, med_out,
     home, start, feat_ref, out_grad_ref, mine_ref, taps_ref, med_ref,
     wt_ref, filt_ref, back_ref, member_ref, ext, short_ref,
-    streams_ref, kv_ref, before_ref, dmix_ref, ds_ref, acc,
+    streams_ref, kv_ref, dmix_ref, ds_ref, acc,
     got, passed, crossed, pieces, stage, landed, ready,
     rim_in, key_in, mix_in, head_ref, tail_in,
     flat_ref, part_ref, sums, gathered, last_ref, last_in, late_ref, late_in,
@@ -48,8 +48,6 @@
     side, row = lax.rem(col, 2), col // 2
     partner = row * 2 + 1 - side
     kind = kv_ref.dtype
-    first = me == 0
-    last = me == n - 1
     barrier = pltpu.get_barrier_semaphore()
 
     def other(d):
@@ -99,8 +97,31 @@
             device_id={"ctx": lax.rem(me + by + n, n)}, device_id_type=MESH,
         )
 
+    def up(copy, begin):
+        if begin:
+            pl.when(me < n - 1)(copy.start)
+        else:
+            pl.when(me < n - 1)(copy.wait_send)
+            pl.when(me > 0)(copy.wait_recv)
+
+    def down(copy, begin):
+        if begin:
+            pl.when(me > 0)(copy.start)
+        else:
+            pl.when(me > 0)(copy.wait_send)
+            pl.when(me < n - 1)(copy.wait_recv)
+
     def key_hop(q):
-        return hop(kv_ref.at[q], key_in.at[q], 1, halo_send.at[0, q], halo_recv.at[0, q])
+        body = pl.ds(GROUP, rows - GROUP)
+        return hop(
+            kv_ref.at[q, body], key_in.at[q, body], 1, halo_send.at[0, q], halo_recv.at[0, q]
+        )
+
+    def key_rest(q):
+        body = pl.ds(0, GROUP)
+        return hop(
+            kv_ref.at[q, body], key_in.at[q, body], 1, halo_send.at[3, q], halo_recv.at[3, q]
+        )
 
     def mix_hop(q):
         return hop(dmix_ref.at[q], mix_in.at[q], -1, halo_send.at[1, q], halo_recv.at[1, q])
@@ -162,6 +183,24 @@
             return carry
 
         lax.fori_loop(low, high, step, 0)
+
+    @pl.when(me == 0)
+    def clear_first():
+        rim_in[...] = jnp.zeros_like(rim_in)
+        key_in[...] = jnp.zeros_like(key_in)
+
+    @pl.when(me == n - 1)
+    def clear_last():
+        mix_in[...] = jnp.zeros_like(mix_in)
+        tail_in[...] = jnp.zeros_like(tail_in)
+
+    pl.semaphore_wait(barrier, n - 1 + half)
+    rim_hop = hop(
+        feat_hbm.at[:, pl.ds(rows - EDGE, EDGE), :], rim_in, 1, rim_sems.at[0], rim_sems.at[1]
+    )
+    up(rim_hop, True)
+    for d in [d for d in range(1, half)] + [0]:
+        chunks(0, nc, lambda q, d=d: pair(d, q).start())
 
     loads[0].wait()
     loads[1].wait()
@@ -173,17 +212,6 @@
     ).astype(kind)
     for s in range(3):
         wt_ref[s, 0:taps] = jnp.dot(taps_ref[s], spread, preferred_element_type=f32)
-    t, s = plane(long_taps, 0), plane(long_taps, 1)
-    turn = jnp.where((t + s == 0) | (t + s == long_taps), 1.0, 0.0).astype(kind)
-    filt_ref[...] = jnp.dot(med_ref[...], turn, preferred_element_type=f32)
-    back_ref[...] = med_ref[...].astype(f32)
-    owned = lax.broadcasted_iota(jnp.int32, (width, long_taps), 0) // GROUP
-    lane = lax.broadcasted_iota(jnp.int32, (width, long_taps), 1)
-    member_ref[0] = jnp.where(owned == lane, 1.0, 0.0).astype(kind)
-    member_ref[1] = jnp.where(owned + groups == lane, 1.0, 0.0).astype(kind)
-    short_ref[...] = jnp.zeros_like(short_ref)
-    last_ref[...] = jnp.zeros_like(last_ref)
-    late_ref[...] = jnp.zeros_like(late_ref)
     loads[2].wait()
 
     def stream(k, cols, count):
@@ -200,30 +228,20 @@
             ext[EDGE : EDGE + rows] = feat_ref[k, :, cols].astype(f32)
             found.append(stream(k, cols, rows))
             streams_ref[k, :, cols] = found[k]
-        kv_ref[q] = (found[1] * found[2]).astype(kind)
-
-    chunks(0, nc, stream_step)
-    pl.semaphore_wait(barrier, n - 1 + half)
-
-    rim_hop = hop(
-        feat_hbm.at[:, pl.ds(rows - EDGE, EDGE), :], rim_in, 1, rim_sems.at[0], rim_sems.at[1]
-    )
-    rim_hop.start()
-    for d in [d for d in range(1, half)] + [0]:
-        chunks(0, nc, lambda q, d=d: pair(d, q).start())
+        kv_ref[q, GROUP:] = (found[1] * found[2])[GROUP:].astype(kind)
+        up(key_hop(q), True)
+        for d in range(1, half):
+            pair(d, q).wait()
+            passed[d, q] = (mine_ref[d, :, cols].astype(f32) + got[d, q].astype(f32)).astype(kind)
+            cross(d, q).start()
 
     for d in range(1, half):
         loads[6 + d].wait()
-
-        def pass_on(q, d=d):
-            pair(d, q).wait()
-            passed[d, q] = (
-                mine_ref[d, :, columns(q)].astype(f32) + got[d, q].astype(f32)
-            ).astype(kind)
-            cross(d, q).start()
-
-        chunks(0, nc, pass_on)
-
+    chunks(0, nc, stream_step)
+    t, s = plane(long_taps, 0), plane(long_taps, 1)
+    turn = jnp.where((t + s == 0) | (t + s == long_taps), 1.0, 0.0).astype(kind)
+    filt_ref[...] = jnp.dot(med_ref[...], turn, preferred_element_type=f32)
+    back_ref[...] = med_ref[...].astype(f32)
     loads[3].wait()
     loads[4].wait()
     loads[6].wait()
@@ -250,13 +268,13 @@
 
         origins = [start[slot] for slot in range(per_device)]
 
-    rim_hop.wait()
+    up(rim_hop, False)
 
     def fill(k, cols, count):
-        ext[0:EDGE] = jnp.where(first, 0.0, rim_in[k, :, cols].astype(f32))
+        ext[0:EDGE] = rim_in[k, :, cols].astype(f32)
         ext[EDGE : EDGE + count] = feat_ref[k, 0:count, cols].astype(f32)
 
-    def send_step(q):
+    def rim_step(q):
         cols = columns(q)
         found = []
         for k in range(3):
@@ -264,24 +282,9 @@
             found.append(stream(k, cols, GROUP))
             streams_ref[k, 0:GROUP, cols] = found[k]
         kv_ref[q, 0:GROUP] = (found[1] * found[2]).astype(kind)
-        key_hop(q).start()
-        pair(0, q).wait()
-        total = mine_ref[0, :, cols].astype(f32) + got[0, q].astype(f32)
-        for d in range(1, half):
-            cross(d, q).wait()
-            total = total + crossed[d, q].astype(f32)
-        for i in range(per_device):
-            pieces[q, i] = total[i * piece_rows : (i + 1) * piece_rows]
-
-        def launch(k):
-            stage[q, k] = pieces[q, pick(lax.rem(me + k, n))].astype(kind)
-            route(q, k).start()
-
-        peers(launch)
-        landed[q, 0] = pieces[q, pick(me)].astype(kind)
-
-    chunks(0, nc, send_step)
-    loads[5].wait()
+        up(key_rest(q), True)
+
+    chunks(0, nc, rim_step)
     owner = lax.broadcasted_iota(jnp.int32, (long_taps, chunk), 1) // GROUP
     flip = jnp.where(t + s == long_taps - 1, 1.0, 0.0).astype(kind)
 
@@ -296,6 +299,41 @@
             product = jnp.dot(table, window, preferred_element_type=f32)
             total = jnp.where(owner == g, product, total)
         return total
+
+    def send_step(q):
+        cols = columns(q)
+        pair(0, q).wait()
+        total = mine_ref[0, :, cols].astype(f32) + got[0, q].astype(f32)
+        for d in range(1, half):
+            cross(d, q).wait()
+            total = total + crossed[d, q].astype(f32)
+        for i in range(per_device):
+            pieces[q, i] = total[i * piece_rows : (i + 1) * piece_rows]
+
+        def launch(k):
+            stage[q, k] = pieces[q, pick(lax.rem(me + k, n))].astype(kind)
+            route(q, k).start()
+
+        peers(launch)
+        landed[q, 0] = pieces[q, pick(me)].astype(kind)
+
+    def mixed_step(q):
+        up(key_hop(q), False)
+        up(key_rest(q), False)
+        window = jnp.concatenate([key_in[q], kv_ref[q]], axis=0)
+        ds_ref[0, :, columns(q)] = banded(filt_ref, q, window, s > t)
+
+    chunks(0, nc, send_step)
+    owned = lax.broadcasted_iota(jnp.int32, (width, long_taps), 0) // GROUP
+    lane = lax.broadcasted_iota(jnp.int32, (width, long_taps), 1)
+    member_ref[0] = jnp.where(owned == lane, 1.0, 0.0).astype(kind)
+    member_ref[1] = jnp.where(owned + groups == lane, 1.0, 0.0).astype(kind)
+    short_ref[...] = jnp.zeros_like(short_ref)
+    last_ref[...] = jnp.zeros_like(last_ref)
+    late_ref[...] = jnp.zeros_like(late_ref)
+    loads[5].wait()
+    mixed_step(0)
+    mixed_step(1)
 
     def short_sums(k, q, value):
         cols = columns(q)
@@ -325,10 +363,8 @@
             acc[slot * piece_rows : (slot + 1) * piece_rows] = ready[at].astype(f32)
         acc[...] = out_grad_ref[:, cols].astype(f32) + acc[...]
         dmix_ref[q] = (acc[...] * streams_ref[0, :, cols]).astype(kind)
-        mix_hop(q).start()
-        key_hop(q).wait()
-        before_ref[...] = jnp.where(first, 0.0, key_in[q].astype(f32)).astype(kind)
-        window = jnp.concatenate([before_ref[...], kv_ref[q]], axis=0)
+        down(mix_hop(q), True)
+        window = jnp.concatenate([key_in[q], kv_ref[q]], axis=0)
         flipped = jnp.dot(flip, dmix_ref[q], preferred_element_type=f32)
         for g in range(near):
             left = jnp.where(owner == g, flipped, 0.0).astype(kind)
@@ -338,7 +374,7 @@
             ring = jnp.where(s + t <= long_taps - 1, both[:, long_taps:], both[:, :long_taps])
             ring = pltpu.roll(ring, 0, 1, stride=1, stride_axis=0)
             lines(g, jnp.sum(ring, axis=0, keepdims=True))
-        value = acc[...] * banded(filt_ref, q, window, s > t)
+        value = acc[...] * ds_ref[0, :, cols]
         ds_ref[0, :, cols] = value
         last_ref[near : near + EDGE] = last_ref[near : near + EDGE] + short_sums(0, q, value)
 
@@ -353,27 +389,34 @@
 
     def back_step(q):
         cols = columns(q)
-        mix_hop(q).wait()
-        after = jnp.where(last, 0.0, mix_in[q].astype(f32)).astype(kind)
-        window = jnp.concatenate([dmix_ref[q], after], axis=0)
+        down(mix_hop(q), False)
+        window = jnp.concatenate([dmix_ref[q], mix_in[q]], axis=0)
         total = banded(back_ref, q, window, s >= t)
         for k in (1, 2):
             value = total * streams_ref[3 - k, :, cols]
             ds_ref[k, :, cols] = value
             late_ref[...] = late_ref[...] + short_sums(k, q, value)
         head_ref[q] = ds_ref[:, 0:EDGE, cols].astype(kind)
-        tail_hop(q).start()
+        down(tail_hop(q), True)
+
+    def feat_rows(k, q, low, tail):
+        cols = columns(q)
+        count = rows - low
+        ext[0:count] = ds_ref[k, low:, cols]
+        ext[count : count + EDGE] = tail
+        total = wt_ref[k, 0:1, cols] * ext[0:count]
+        for lag in range(1, taps):
+            total = total + wt_ref[k, lag : lag + 1, cols] * ext[lag : lag + count]
+        feat_out[k, low:, cols] = total.astype(feat_out.dtype)
 
     def feat_step(q):
-        cols = columns(q)
-        tail_hop(q).wait()
         for k in range(3):
-            ext[0:rows] = ds_ref[k, :, cols]
-            ext[rows:] = jnp.where(last, 0.0, tail_in[q, k].astype(f32))
-            total = wt_ref[k, 0:1, cols] * ds_ref[k, :, cols]
-            for lag in range(1, taps):
-                total = total + wt_ref[k, lag : lag + 1, cols] * ext[lag : lag + rows]
-            feat_out[k, :, cols] = total.astype(feat_out.dtype)
+            feat_rows(k, q, 0, jnp.zeros((EDGE, chunk), f32))
+
+    def tail_step(q):
+        down(tail_hop(q), False)
+        for k in range(3):
+            feat_rows(k, q, rows - GROUP, tail_in[q, k].astype(f32))
 
     share = part_ref.shape[1]
     used = (nc - 1) * near
@@ -381,6 +424,7 @@
     early(0)
 
     def both_steps(q):
+        mixed_step(q + 1)
         early(q)
         back_step(q - 1)
 
@@ -393,15 +437,18 @@
     sums[0] = part_ref[me]
     receive(nc - 1, final_lines)
     peers(lambda k: share_last(k).start())
+    back_step(nc - 2)
+    chunks(0, nc - 2, feat_step)
     peers(lambda k: scatter(k).wait())
     result = sums[0]
     for k in range(1, n):
         result = result + sums[k]
     gathered[me] = result
     peers(lambda k: gather(k).start())
-    chunks(nc - 2, nc, back_step)
+    back_step(nc - 1)
     peers(lambda k: share_late(k).start())
-    chunks(0, nc, feat_step)
+    chunks(nc - 2, nc, feat_step)
+    chunks(0, nc, tail_step)
     peers(lambda k: gather(k).wait())
     for k in range(n):
         flat_ref[k * share : (k + 1) * share] = gathered[k]
@@ -501,7 +548,7 @@
             pltpu.VMEM((3, 8, width), f32), pltpu.VMEM((groups, taps), f32),
             pltpu.VMEM((groups, taps), f32), pltpu.VMEM((2, width, taps), half),
             pltpu.VMEM((rows + EDGE, chunk), f32), pltpu.VMEM((EDGE, chunk), f32),
-            wide, held, pltpu.VMEM((rows, chunk), half), held, wide,
+            wide, held, held, wide,
             pltpu.VMEM((rows, chunk), f32),
             crossing, crossing, crossing,
             pltpu.VMEM((nc, per_device, piece_rows, chunk), f32), routed, routed,
@@ -511,7 +558,7 @@
             pltpu.VMEM((near + EDGE, taps), f32), pltpu.VMEM((ctx_count, near + EDGE, taps), f32),
             pltpu.VMEM((EDGE, taps), f32), pltpu.VMEM((ctx_count, EDGE, taps), f32),
             dma((6 + tp_count // 2,)), flags, flags, flags, flags, lanes, lanes,
-            dma((2,)), dma((3, nc)), dma((3, nc)),
+            dma((2,)), dma((4, nc)), dma((4, nc)),
             peers, peers, peers, peers, peers, peers, peers, peers,
         ],
         compiler_params=pltpu.CompilerParams(

time: 45 us -> 41.3 us (0.918)
  Pallas kernels: 44.2 us -> 40.5 us
    pallas_call x1, Pallas kernels: 43.3 us -> 39.6 us  [shards(): pl.pallas_call(functools.partial(whole_kernel, ctx_count, tp_count, inlin...]
where the time goes in v2:
time: 41.3 us; the launch traced here: 41.1 us
  Pallas kernels  40.5 us (98%)
  between operations  0.64 us (2%)
    pallas_call x1, Pallas kernels, shards(): pl.pallas_call(functools.partial(whole_kernel, ctx_count, tp_count, inlin...  39.6 us
    pallas_call x1, Pallas kernels, shards(): pl.pallas_call(store_kernel, in_specs=[vmem] * 3, out_specs=(hbm,) * 3, o...  0.91 us

profile of v2, /device:TPU:0, one launch (start us, length us, event | category | flops | bytes accessed | tf_op | source)
XLA Modules:
  0.0 41.1 jit_solution(9855866786285969774)
XLA Ops:
  0.6 39.6 %shard_map.94 = (bf16[3,128,1024]{2,1,0:T(8,128)(2,1)S(1)}, f32[3,7,64]{2,1,0:T(8,128)S(1)}, f32[64,128]{1,0:T(8,128)S(1)}) custom-call(s32[32]{0:T(128)} %home_hbm.1, s32[32]{0:T(128)} %start_hbm.1, bf16[128,4096]{1,0:T(8,128)(2,1)} %bitcast.3, bf16[3,128,1024]{2,1,0:T(8,128)(2,1)} %feat_hbm.1, bf16[128,1024]{1,0:T(8,128)(2,1)} %grad_hbm.1, ...), custom_call_target="tpu_custom_call" | custom-call | flops 3221225472 | bytes 5242880 | tf_op jit(solution)/shard_map/pallas_call | solution.py:538
  40.2 0.9 %shard_map.95 = (bf16[3,128,1024]{2,1,0:T(8,128)(2,1)}, f32[3,7,64]{2,1,0:T(8,128)}, f32[64,128]{1,0:T(8,128)}) custom-call(bf16[3,128,1024]{2,1,0:T(8,128)(2,1)S(1)} %get-tuple-element.9.feat_ref, f32[3,7,64]{2,1,0:T(8,128)S(1)} %get-tuple-element.10.short_ref, f32[64,128]{1,0:T(8,128)S(1)} %get-tuple-element.11.med_ref), custom_call_target="tpu_custom_call" | custom-call | bytes 1048576 | tf_op jit(solution)/shard_map/pallas_call | solution.py:577

commit v3 on v2

--- a/solution.py
+++ b/solution.py
@@ -314,7 +314,7 @@
             stage[q, k] = pieces[q, pick(lax.rem(me + k, n))].astype(kind)
             route(q, k).start()
 
-        peers(launch)
+        peers(lambda j: launch(n - j))
         landed[q, 0] = pieces[q, pick(me)].astype(kind)
 
     def mixed_step(q):
@@ -332,8 +332,7 @@
     last_ref[...] = jnp.zeros_like(last_ref)
     late_ref[...] = jnp.zeros_like(late_ref)
     loads[5].wait()
-    mixed_step(0)
-    mixed_step(1)
+    chunks(0, nc - 1, mixed_step)
 
     def short_sums(k, q, value):
         cols = columns(q)
@@ -354,7 +353,7 @@
             )
         return found
 
-    def receive(q, lines):
+    def receive(q):
         cols = columns(q)
         peers(lambda k: route(q, k).wait())
         ready[...] = landed[q]
@@ -364,6 +363,9 @@
         acc[...] = out_grad_ref[:, cols].astype(f32) + acc[...]
         dmix_ref[q] = (acc[...] * streams_ref[0, :, cols]).astype(kind)
         down(mix_hop(q), True)
+
+    def lag_step(q, lines):
+        cols = columns(q)
         window = jnp.concatenate([key_in[q], kv_ref[q]], axis=0)
         flipped = jnp.dot(flip, dmix_ref[q], preferred_element_type=f32)
         for g in range(near):
@@ -378,11 +380,11 @@
         ds_ref[0, :, cols] = value
         last_ref[near : near + EDGE] = last_ref[near : near + EDGE] + short_sums(0, q, value)
 
-    def early(q):
+    def early_lags(q):
         def lines(g, line):
             flat_ref[pl.ds(q * near + g, 1), :] = line
 
-        receive(q, lines)
+        lag_step(q, lines)
 
     def final_lines(g, line):
         last_ref[g : g + 1] = line
@@ -421,24 +423,30 @@
     share = part_ref.shape[1]
     used = (nc - 1) * near
 
-    early(0)
+    receive(0)
+    early_lags(0)
+    receive(1)
+    mixed_step(nc - 1)
+    early_lags(1)
 
     def both_steps(q):
-        mixed_step(q + 1)
-        early(q)
-        back_step(q - 1)
-
-    chunks(1, nc - 1, both_steps)
+        receive(q)
+        back_step(q - 2)
+        early_lags(q)
+
+    chunks(2, nc - 1, both_steps)
     if n * share > used:
         flat_ref[used : n * share] = jnp.zeros((n * share - used, long_taps), f32)
     for k in range(n):
         part_ref[k] = flat_ref[k * share : (k + 1) * share]
     peers(lambda k: scatter(k).start())
     sums[0] = part_ref[me]
-    receive(nc - 1, final_lines)
+    receive(nc - 1)
+    back_step(nc - 3)
+    lag_step(nc - 1, final_lines)
     peers(lambda k: share_last(k).start())
     back_step(nc - 2)
-    chunks(0, nc - 2, feat_step)
+    feat_step(0)
     peers(lambda k: scatter(k).wait())
     result = sums[0]
     for k in range(1, n):
@@ -447,7 +455,7 @@
     peers(lambda k: gather(k).start())
     back_step(nc - 1)
     peers(lambda k: share_late(k).start())
-    chunks(nc - 2, nc, feat_step)
+    chunks(1, nc, feat_step)
     chunks(0, nc, tail_step)
     peers(lambda k: gather(k).wait())
     for k in range(n):

time: 41.3 us -> 39.6 us (0.959)
  Pallas kernels: 40.5 us -> 38.8 us
    pallas_call x1, Pallas kernels: 39.6 us -> 37.9 us  [shards(): pl.pallas_call(functools.partial(whole_kernel, ctx_count, tp_count, inlin...]
where the time goes in v3:
time: 39.6 us; the launch traced here: 39.5 us
  Pallas kernels  38.8 us (98%)
  between operations  0.64 us (2%)
    pallas_call x1, Pallas kernels, shards(): pl.pallas_call(functools.partial(whole_kernel, ctx_count, tp_count, inlin...  37.9 us
    pallas_call x1, Pallas kernels, shards(): pl.pallas_call(store_kernel, in_specs=[vmem] * 3, out_specs=(hbm,) * 3, o...  0.91 us

profile of v3, /device:TPU:0, one launch (start us, length us, event | category | flops | bytes accessed | tf_op | source)
XLA Modules:
  0.0 39.5 jit_solution(11010167537709582671)
XLA Ops:
  0.6 37.9 %shard_map.94 = (bf16[3,128,1024]{2,1,0:T(8,128)(2,1)S(1)}, f32[3,7,64]{2,1,0:T(8,128)S(1)}, f32[64,128]{1,0:T(8,128)S(1)}) custom-call(s32[32]{0:T(128)} %home_hbm.1, s32[32]{0:T(128)} %start_hbm.1, bf16[128,4096]{1,0:T(8,128)(2,1)} %bitcast.3, bf16[3,128,1024]{2,1,0:T(8,128)(2,1)} %feat_hbm.1, bf16[128,1024]{1,0:T(8,128)(2,1)} %grad_hbm.1, ...), custom_call_target="tpu_custom_call" | custom-call | flops 3221225472 | bytes 5242880 | tf_op jit(solution)/shard_map/pallas_call | solution.py:546
  38.5 0.9 %shard_map.95 = (bf16[3,128,1024]{2,1,0:T(8,128)(2,1)}, f32[3,7,64]{2,1,0:T(8,128)}, f32[64,128]{1,0:T(8,128)}) custom-call(bf16[3,128,1024]{2,1,0:T(8,128)(2,1)S(1)} %get-tuple-element.9.feat_ref, f32[3,7,64]{2,1,0:T(8,128)S(1)} %get-tuple-element.10.short_ref, f32[64,128]{1,0:T(8,128)S(1)} %get-tuple-element.11.med_ref), custom_call_target="tpu_custom_call" | custom-call | bytes 1048576 | tf_op jit(solution)/shard_map/pallas_call | solution.py:585

commit v4 on v3

--- a/solution.py
+++ b/solution.py
@@ -27,7 +27,7 @@
     home_hbm, start_hbm, attn_hbm, feat_hbm, grad_hbm, taps_hbm, med_hbm,
     feat_out, short_out, med_out,
     home, start, feat_ref, out_grad_ref, mine_ref, taps_ref, med_ref,
-    wt_ref, filt_ref, back_ref, member_ref, ext, short_ref,
+    wt_ref, filt_ref, back_ref, member_ref, wide_ref, short_ref,
     streams_ref, kv_ref, dmix_ref, ds_ref, acc,
     got, passed, crossed, pieces, stage, landed, ready,
     rim_in, key_in, mix_in, head_ref, tail_in,
@@ -58,7 +58,7 @@
             act(k)
             return carry
 
-        lax.fori_loop(1, n, step, 0)
+        lax.fori_loop(1, n, step, 0, unroll=inline)
 
     def greet(k):
         pl.semaphore_signal(
@@ -76,20 +76,17 @@
     def part(which, q):
         return pl.ds(pl.multiple_of(which * width + q * chunk, chunk), chunk)
 
+    def load(source, target, at):
+        return pltpu.make_async_copy(source, target, local.at[at])
+
     loads = [
-        pltpu.make_async_copy(source, target, local.at[i])
-        for i, (source, target) in enumerate(
-            [
-                (taps_hbm, taps_ref), (med_hbm, med_ref), (feat_hbm, feat_ref),
-                (home_hbm, home), (start_hbm, start), (grad_hbm, out_grad_ref),
-            ]
-            + [
-                (attn_hbm.at[:, slab(other(d))], mine_ref.at[d]) for d in range(half)
-            ]
-        )
+        load(taps_hbm, taps_ref, 0), load(med_hbm, med_ref, 1), load(feat_hbm, feat_ref, 2),
+        load(home_hbm, home, 3), load(start_hbm, start, 4), load(grad_hbm, out_grad_ref, 5),
+    ] + [
+        load(attn_hbm.at[:, slab(other(d))], mine_ref.at[d], 6 + d) for d in range(half)
     ]
-    for load in loads:
-        load.start()
+    for at in [6 + d for d in range(1, half)] + [0, 2]:
+        loads[at].start()
 
     def hop(source, target, by, sends, recvs):
         return pltpu.make_async_remote_copy(
@@ -201,9 +198,11 @@
     up(rim_hop, True)
     for d in [d for d in range(1, half)] + [0]:
         chunks(0, nc, lambda q, d=d: pair(d, q).start())
-
+    for at in (1, 6, 3, 4, 5):
+        loads[at].start()
+
+    wide_ref[:, 0:EDGE] = jnp.zeros((3, EDGE, width), f32)
     loads[0].wait()
-    loads[1].wait()
     spread = jnp.where(
         lax.broadcasted_iota(jnp.int32, (groups, width), 0)
         == lax.broadcasted_iota(jnp.int32, (groups, width), 1) // GROUP,
@@ -215,17 +214,17 @@
     loads[2].wait()
 
     def stream(k, cols, count):
-        total = wt_ref[k, 0:1, cols] * ext[EDGE : EDGE + count]
+        total = wt_ref[k, 0:1, cols] * wide_ref[k, EDGE : EDGE + count, cols]
         for lag in range(1, taps):
-            total = total + wt_ref[k, lag : lag + 1, cols] * ext[EDGE - lag : EDGE - lag + count]
+            rows_back = wide_ref[k, EDGE - lag : EDGE - lag + count, cols]
+            total = total + wt_ref[k, lag : lag + 1, cols] * rows_back
         return total
 
     def stream_step(q):
         cols = columns(q)
         found = []
         for k in range(3):
-            ext[0:EDGE] = jnp.zeros((EDGE, chunk), f32)
-            ext[EDGE : EDGE + rows] = feat_ref[k, :, cols].astype(f32)
+            wide_ref[k, EDGE : EDGE + rows, cols] = feat_ref[k, :, cols].astype(f32)
             found.append(stream(k, cols, rows))
             streams_ref[k, :, cols] = found[k]
         kv_ref[q, GROUP:] = (found[1] * found[2])[GROUP:].astype(kind)
@@ -239,6 +238,7 @@
         loads[6 + d].wait()
     chunks(0, nc, stream_step)
     t, s = plane(long_taps, 0), plane(long_taps, 1)
+    loads[1].wait()
     turn = jnp.where((t + s == 0) | (t + s == long_taps), 1.0, 0.0).astype(kind)
     filt_ref[...] = jnp.dot(med_ref[...], turn, preferred_element_type=f32)
     back_ref[...] = med_ref[...].astype(f32)
@@ -270,15 +270,11 @@
 
     up(rim_hop, False)
 
-    def fill(k, cols, count):
-        ext[0:EDGE] = rim_in[k, :, cols].astype(f32)
-        ext[EDGE : EDGE + count] = feat_ref[k, 0:count, cols].astype(f32)
-
     def rim_step(q):
         cols = columns(q)
         found = []
         for k in range(3):
-            fill(k, cols, GROUP)
+            wide_ref[k, 0:EDGE, cols] = rim_in[k, :, cols].astype(f32)
             found.append(stream(k, cols, GROUP))
             streams_ref[k, 0:GROUP, cols] = found[k]
         kv_ref[q, 0:GROUP] = (found[1] * found[2]).astype(kind)
@@ -321,7 +317,7 @@
         up(key_hop(q), False)
         up(key_rest(q), False)
         window = jnp.concatenate([key_in[q], kv_ref[q]], axis=0)
-        ds_ref[0, :, columns(q)] = banded(filt_ref, q, window, s > t)
+        ds_ref[0, 0:rows, columns(q)] = banded(filt_ref, q, window, s > t)
 
     chunks(0, nc, send_step)
     owned = lax.broadcasted_iota(jnp.int32, (width, long_taps), 0) // GROUP
@@ -331,15 +327,15 @@
     short_ref[...] = jnp.zeros_like(short_ref)
     last_ref[...] = jnp.zeros_like(last_ref)
     late_ref[...] = jnp.zeros_like(late_ref)
+    ds_ref[:, rows:] = jnp.zeros((3, EDGE, width), f32)
     loads[5].wait()
     chunks(0, nc - 1, mixed_step)
 
     def short_sums(k, q, value):
         cols = columns(q)
-        fill(k, cols, rows)
         for lag in range(taps):
             short_ref[lag : lag + 1] = jnp.sum(
-                value * ext[EDGE - lag : EDGE - lag + rows], axis=0, keepdims=True
+                value * wide_ref[k, EDGE - lag : EDGE - lag + rows, cols], axis=0, keepdims=True
             )
         exact = short_ref[...]
         high = exact.astype(kind)
@@ -376,8 +372,8 @@
             ring = jnp.where(s + t <= long_taps - 1, both[:, long_taps:], both[:, :long_taps])
             ring = pltpu.roll(ring, 0, 1, stride=1, stride_axis=0)
             lines(g, jnp.sum(ring, axis=0, keepdims=True))
-        value = acc[...] * ds_ref[0, :, cols]
-        ds_ref[0, :, cols] = value
+        value = acc[...] * ds_ref[0, 0:rows, cols]
+        ds_ref[0, 0:rows, cols] = value
         last_ref[near : near + EDGE] = last_ref[near : near + EDGE] + short_sums(0, q, value)
 
     def early_lags(q):
@@ -396,29 +392,27 @@
         total = banded(back_ref, q, window, s >= t)
         for k in (1, 2):
             value = total * streams_ref[3 - k, :, cols]
-            ds_ref[k, :, cols] = value
+            ds_ref[k, 0:rows, cols] = value
             late_ref[...] = late_ref[...] + short_sums(k, q, value)
         head_ref[q] = ds_ref[:, 0:EDGE, cols].astype(kind)
         down(tail_hop(q), True)
 
-    def feat_rows(k, q, low, tail):
-        cols = columns(q)
-        count = rows - low
-        ext[0:count] = ds_ref[k, low:, cols]
-        ext[count : count + EDGE] = tail
-        total = wt_ref[k, 0:1, cols] * ext[0:count]
+    def feat_rows(k, q, low):
+        cols = columns(q)
+        total = wt_ref[k, 0:1, cols] * ds_ref[k, low:rows, cols]
         for lag in range(1, taps):
-            total = total + wt_ref[k, lag : lag + 1, cols] * ext[lag : lag + count]
+            total = total + wt_ref[k, lag : lag + 1, cols] * ds_ref[k, low + lag : rows + lag, cols]
         feat_out[k, low:, cols] = total.astype(feat_out.dtype)
 
     def feat_step(q):
         for k in range(3):
-            feat_rows(k, q, 0, jnp.zeros((EDGE, chunk), f32))
+            feat_rows(k, q, 0)
 
     def tail_step(q):
         down(tail_hop(q), False)
         for k in range(3):
-            feat_rows(k, q, rows - GROUP, tail_in[q, k].astype(f32))
+            ds_ref[k, rows:, columns(q)] = tail_in[q, k].astype(f32)
+            feat_rows(k, q, rows - GROUP)
 
     share = part_ref.shape[1]
     used = (nc - 1) * near
@@ -443,10 +437,9 @@
     sums[0] = part_ref[me]
     receive(nc - 1)
     back_step(nc - 3)
+    back_step(nc - 2)
     lag_step(nc - 1, final_lines)
     peers(lambda k: share_last(k).start())
-    back_step(nc - 2)
-    feat_step(0)
     peers(lambda k: scatter(k).wait())
     result = sums[0]
     for k in range(1, n):
@@ -455,7 +448,7 @@
     peers(lambda k: gather(k).start())
     back_step(nc - 1)
     peers(lambda k: share_late(k).start())
-    chunks(1, nc, feat_step)
+    chunks(0, nc, feat_step)
     chunks(0, nc, tail_step)
     peers(lambda k: gather(k).wait())
     for k in range(n):
@@ -532,6 +525,7 @@
     parts = pltpu.VMEM((ctx_count, share, taps), f32)
     held = pltpu.VMEM((nc, rows, chunk), half)
     wide = pltpu.VMEM((3, rows, width), f32)
+    padded = pltpu.VMEM((3, rows + EDGE, width), f32)
     crossing = pltpu.VMEM((tp_count // 2, nc, rows, chunk), half)
     routed = pltpu.VMEM((nc, ctx_count, piece_rows, chunk), half)
     heads = pltpu.VMEM((nc, 3, EDGE, chunk), half)
@@ -555,8 +549,8 @@
             pltpu.VMEM((3, short_taps, groups), half), pltpu.VMEM((groups, taps), half),
             pltpu.VMEM((3, 8, width), f32), pltpu.VMEM((groups, taps), f32),
             pltpu.VMEM((groups, taps), f32), pltpu.VMEM((2, width, taps), half),
-            pltpu.VMEM((rows + EDGE, chunk), f32), pltpu.VMEM((EDGE, chunk), f32),
-            wide, held, held, wide,
+            padded, pltpu.VMEM((EDGE, chunk), f32),
+            wide, held, held, padded,
             pltpu.VMEM((rows, chunk), f32),
             crossing, crossing, crossing,
             pltpu.VMEM((nc, per_device, piece_rows, chunk), f32), routed, routed,

time: 39.6 us -> 39.4 us (level)
  no operation moved by 1% of the time
where the time goes in v4:
time: 39.4 us; the launch traced here: 39.2 us
  Pallas kernels  38.6 us (98%)
  between operations  0.64 us (2%)
    pallas_call x1, Pallas kernels, shards(): pl.pallas_call(functools.partial(whole_kernel, ctx_count, tp_count, inlin...  37.7 us
    pallas_call x1, Pallas kernels, shards(): pl.pallas_call(store_kernel, in_specs=[vmem] * 3, out_specs=(hbm,) * 3, o...  0.91 us

profile of v4, /device:TPU:0, one launch (start us, length us, event | category | flops | bytes accessed | tf_op | source)
XLA Modules:
  0.0 39.2 jit_solution(6692287501437467939)
XLA Ops:
  0.6 37.7 %shard_map.94 = (bf16[3,128,1024]{2,1,0:T(8,128)(2,1)S(1)}, f32[3,7,64]{2,1,0:T(8,128)S(1)}, f32[64,128]{1,0:T(8,128)S(1)}) custom-call(s32[32]{0:T(128)} %home_hbm.1, s32[32]{0:T(128)} %start_hbm.1, bf16[128,4096]{1,0:T(8,128)(2,1)} %bitcast.3, bf16[3,128,1024]{2,1,0:T(8,128)(2,1)} %feat_hbm.1, bf16[128,1024]{1,0:T(8,128)(2,1)} %grad_hbm.1, ...), custom_call_target="tpu_custom_call" | custom-call | flops 3221225472 | bytes 5242880 | tf_op jit(solution)/shard_map/pallas_call | solution.py:540
  38.3 0.9 %shard_map.95 = (bf16[3,128,1024]{2,1,0:T(8,128)(2,1)}, f32[3,7,64]{2,1,0:T(8,128)}, f32[64,128]{1,0:T(8,128)}) custom-call(bf16[3,128,1024]{2,1,0:T(8,128)(2,1)S(1)} %get-tuple-element.9.feat_ref, f32[3,7,64]{2,1,0:T(8,128)S(1)} %get-tuple-element.10.short_ref, f32[64,128]{1,0:T(8,128)S(1)} %get-tuple-element.11.med_ref), custom_call_target="tpu_custom_call" | custom-call | bytes 1048576 | tf_op jit(solution)/shard_map/pallas_call | solution.py:579

commit v5 on v4

--- a/solution.py
+++ b/solution.py
@@ -385,7 +385,7 @@
     def final_lines(g, line):
         last_ref[g : g + 1] = line
 
-    def back_step(q):
+    def back_step(q, final=False):
         cols = columns(q)
         down(mix_hop(q), False)
         window = jnp.concatenate([dmix_ref[q], mix_in[q]], axis=0)
@@ -394,6 +394,8 @@
             value = total * streams_ref[3 - k, :, cols]
             ds_ref[k, 0:rows, cols] = value
             late_ref[...] = late_ref[...] + short_sums(k, q, value)
+        if final:
+            peers(lambda k: share_late(k).start())
         head_ref[q] = ds_ref[:, 0:EDGE, cols].astype(kind)
         down(tail_hop(q), True)
 
@@ -446,8 +448,7 @@
         result = result + sums[k]
     gathered[me] = result
     peers(lambda k: gather(k).start())
-    back_step(nc - 1)
-    peers(lambda k: share_late(k).start())
+    back_step(nc - 1, final=True)
     chunks(0, nc, feat_step)
     chunks(0, nc, tail_step)
     peers(lambda k: gather(k).wait())

time: 39.4 us -> 39.3 us (level)
  no operation moved by 1% of the time
where the time goes in v5:
time: 39.3 us; the launch traced here: 39.1 us
  Pallas kernels  38.5 us (98%)
  between operations  0.64 us (2%)
    pallas_call x1, Pallas kernels, shards(): pl.pallas_call(functools.partial(whole_kernel, ctx_count, tp_count, inlin...  37.6 us
    pallas_call x1, Pallas kernels, shards(): pl.pallas_call(store_kernel, in_specs=[vmem] * 3, out_specs=(hbm,) * 3, o...  0.91 us

profile of v5, /device:TPU:0, one launch (start us, length us, event | category | flops | bytes accessed | tf_op | source)
XLA Modules:
  0.0 39.1 jit_solution(18350780690914238159)
XLA Ops:
  0.6 37.6 %shard_map.94 = (bf16[3,128,1024]{2,1,0:T(8,128)(2,1)S(1)}, f32[3,7,64]{2,1,0:T(8,128)S(1)}, f32[64,128]{1,0:T(8,128)S(1)}) custom-call(s32[32]{0:T(128)} %home_hbm.1, s32[32]{0:T(128)} %start_hbm.1, bf16[128,4096]{1,0:T(8,128)(2,1)} %bitcast.3, bf16[3,128,1024]{2,1,0:T(8,128)(2,1)} %feat_hbm.1, bf16[128,1024]{1,0:T(8,128)(2,1)} %grad_hbm.1, ...), custom_call_target="tpu_custom_call" | custom-call | flops 3221225472 | bytes 5242880 | tf_op jit(solution)/shard_map/pallas_call | solution.py:541
  38.2 0.9 %shard_map.95 = (bf16[3,128,1024]{2,1,0:T(8,128)(2,1)}, f32[3,7,64]{2,1,0:T(8,128)}, f32[64,128]{1,0:T(8,128)}) custom-call(bf16[3,128,1024]{2,1,0:T(8,128)(2,1)S(1)} %get-tuple-element.9.feat_ref, f32[3,7,64]{2,1,0:T(8,128)S(1)} %get-tuple-element.10.short_ref, f32[64,128]{1,0:T(8,128)S(1)} %get-tuple-element.11.med_ref), custom_call_target="tpu_custom_call" | custom-call | bytes 1048576 | tf_op jit(solution)/shard_map/pallas_call | solution.py:580
